TPU v7x, 32 devices: a whole 2x2x4 slice. The times are simulated.
32 devices in a mesh: cell: 8 (over z, x), desc: 4 (over y, core).
Axes of the slice: x: 2, y: 2, z: 4, core: 2. Of those that a mesh axis runs over, the one named last changes fastest.
Arguments:
- cells: float32 [8192, 256], P('cell'), may hold values from -128 to 128
- descs: float32 [8192, 256], P('desc'), may hold values from -4 to 4
- g_start: float32 [8192], P('desc'), may hold values from -8 to 8
- cot_f: float32 [8192], P('cell'), may hold values from -24 to 24
- cot_g: float32 [8192], P('desc'), may hold values from -24 to 24
Outputs:
- grad_cells: float32 [8192, 256], P('cell')
- grad_descs: float32 [8192, 256], P('desc')
All inputs are finite; a program needn't handle non-finite values.
Results may differ from a plain program's by a relative error of at most 0.0003.
Values sent between devices are 32-bit elements; how exact they have to be, the bound alone decides.
A program may use at most 192 MiB of HBM per device.

v0:
```python
import math

import jax
import jax.numpy as jnp
from jax import lax
from jax.sharding import PartitionSpec as P

ITERS = 4


def combined_all(value, axis, join):
    pieces = jax.tree.map(lambda part: lax.all_gather(part, axis), value)
    head = jax.tree.map(lambda part: part[0], pieces)
    tail = jax.tree.map(lambda part: part[1:], pieces)
    so_far, _ = lax.scan(lambda so_far, share: (join(so_far, share), None), head, tail)
    return so_far


def lse_merge(first, second):
    max_one, sum_one = first
    max_two, sum_two = second
    top = jnp.maximum(max_one, max_two)
    return (top, sum_one * jnp.exp(max_one - top) + sum_two * jnp.exp(max_two - top))


def plan_adjoint(xrows, ycols, g_first, cf_rows, cg_cols, over_rows, over_cols, sum_rows, sum_cols):
    scale = 2.0 / math.sqrt(xrows.shape[1])
    highest = lax.Precision.HIGHEST
    logit = (
        lax.dot_general(
            xrows,
            ycols,
            (((1,), (1,)), ((), ())),
            precision=highest,
            preferred_element_type=jnp.float32,
        )
        * scale
    )
    g_now = g_first
    f_list = []
    g_list = [g_first]
    for step in range(ITERS):
        zvals = logit + g_now[None, :]
        row_max = jnp.max(zvals, axis=1)
        row_sum = jnp.sum(jnp.exp(zvals - row_max[:, None]), axis=1)
        row_max, row_sum = over_rows(row_max, row_sum)
        f_now = -(row_max + jnp.log(row_sum))
        wvals = logit + f_now[:, None]
        col_max = jnp.max(wvals, axis=0)
        col_sum = jnp.sum(jnp.exp(wvals - col_max[None, :]), axis=0)
        col_max, col_sum = over_cols(col_max, col_sum)
        g_now = -(col_max + jnp.log(col_sum))
        f_list.append(f_now)
        g_list.append(g_now)
    gbar = cg_cols
    lbar = jnp.zeros_like(logit)
    for step in reversed(range(ITERS)):
        g_here = g_list[step + 1]
        bplan = jnp.exp(logit + f_list[step][:, None] + g_here[None, :])
        fbar = -sum_rows(jnp.sum(bplan * gbar[None, :], axis=1))
        if step == ITERS - 1:
            fbar = fbar + cf_rows
        aplan = bplan * jnp.exp(g_list[step] - g_here)[None, :]
        lbar = lbar - (bplan * gbar[None, :] + aplan * fbar[:, None])
        if step > 0:
            gbar = -sum_cols(jnp.sum(aplan * fbar[:, None], axis=0))
    return (lbar, scale)


def on_device(cells, descs, g_start, cot_f, cot_g):
    highest = lax.Precision.HIGHEST
    lbar, scale = plan_adjoint(
        cells,
        descs,
        g_start,
        cot_f,
        cot_g,
        lambda big, total: combined_all((big, total), "desc", lse_merge),
        lambda big, total: combined_all((big, total), "cell", lse_merge),
        lambda part: lax.psum(part, "desc"),
        lambda part: lax.psum(part, "cell"),
    )
    part_x = scale * jnp.dot(lbar, descs, precision=highest, preferred_element_type=jnp.float32)
    part_y = scale * lax.dot_general(
        lbar, cells, (((0,), (0,)), ((), ())), precision=highest, preferred_element_type=jnp.float32
    )
    grad_cells = lax.psum(part_x, "desc")
    grad_descs = lax.psum(part_y, "cell")
    return (grad_cells, grad_descs)


def solution(mesh):
    placed = (P("cell", None), P("desc", None), P("desc"), P("cell"), P("desc"))
    return jax.shard_map(
        on_device,
        mesh=mesh,
        in_specs=placed,
        out_specs=(P("cell", None), P("desc", None)),
        check_vma=False,
    )
```

profile of v0, /device:TPU:27, one launch (start us, length us, event | category | flops | bytes accessed | tf_op | source)
XLA Modules:
  0.0 667.5 jit_solution(9534914086355051639)
XLA Ops:
  7.2 1.5 copy-done
  8.8 9.0 %add_reduce_fusion.3 = (f32[1024]{0:T(1024)S(1)}, f32[1024,2048]{1,0:T(8,128)S(1)}) fusion(f32[2048]{0:T(1024)} %param.23, f32[1024,256]{1,0:T(8,128)} %param.21, f32[2048,256]{1,0:T(8,128)S(1)} %copy-done), kind=kOutput, calls=%fused_computation.47 | convolution fusion | flops 6448741376 | bytes 11546624 | tf_op jit(solution)/shard_map/dot_general | solution.py:30
  17.8 5.7 all-gather
  23.5 2.0 exponential_reduce_fusion.7
  25.5 5.2 all-gather.1
  30.7 0.2 while.96
  30.9 4.2 add_reduce_fusion.7
  35.1 1.6 copy-done.2
  36.7 1.8 exponential_reduce_fusion.6
  38.5 24.5 %all-gather.2 = f32[16384]{0:T(1024)S(1)} all-gather(f32[2048]{0:T(1024)S(1)} %add_reduce_fusion.7), channel_id=4, replica_groups=mesh['cell'=8,'desc'=4] {'cell'}, dimensions={0}, use_global_device_ids=true | all-gather | bytes 73728 | tf_op jit(solution)/shard_map/all_gather | solution.py:12
  63.0 24.6 %all-gather.3 = f32[16384]{0:T(1024)S(1)} all-gather(f32[2048]{0:T(1024)S(1)} %exponential_reduce_fusion.6), channel_id=5, replica_groups=mesh['cell'=8,'desc'=4] {'cell'}, dimensions={0}, use_global_device_ids=true | all-gather | bytes 73728 | tf_op jit(solution)/shard_map/all_gather | solution.py:12
  87.6 0.4 while.97
  88.1 4.0 add_reduce_fusion.2
  92.1 4.4 exponential_reduce_fusion.5
  96.5 17.6 %all-gather.4 = f32[4096]{0:T(1024)S(1)} all-gather(f32[1024]{0:T(1024)S(1)} %add_reduce_fusion.2), channel_id=6, replica_groups=mesh['cell'=8,'desc'=4] {'desc'}, dimensions={0}, use_global_device_ids=true | all-gather | bytes 20480 | tf_op jit(solution)/shard_map/all_gather | solution.py:12
  114.1 5.2 all-gather.5
  119.3 0.2 while.98
  119.5 4.0 add_reduce_fusion.6
  123.5 4.3 exponential_reduce_fusion.4
  127.8 24.4 %all-gather.6 = f32[16384]{0:T(1024)S(1)} all-gather(f32[2048]{0:T(1024)S(1)} %add_reduce_fusion.6), channel_id=8, replica_groups=mesh['cell'=8,'desc'=4] {'cell'}, dimensions={0}, use_global_device_ids=true | all-gather | bytes 73728 | tf_op jit(solution)/shard_map/all_gather | solution.py:12
  152.3 24.3 %all-gather.7 = f32[16384]{0:T(1024)S(1)} all-gather(f32[2048]{0:T(1024)S(1)} %exponential_reduce_fusion.4), channel_id=9, replica_groups=mesh['cell'=8,'desc'=4] {'cell'}, dimensions={0}, use_global_device_ids=true | all-gather | bytes 73728 | tf_op jit(solution)/shard_map/all_gather | solution.py:12
  176.6 0.4 while.99
  177.0 4.0 add_reduce_fusion.1
  181.0 4.4 exponential_reduce_fusion.3
  185.4 17.6 %all-gather.8 = f32[4096]{0:T(1024)S(1)} all-gather(f32[1024]{0:T(1024)S(1)} %add_reduce_fusion.1), channel_id=10, replica_groups=mesh['cell'=8,'desc'=4] {'desc'}, dimensions={0}, use_global_device_ids=true | all-gather | bytes 20480 | tf_op jit(solution)/shard_map/all_gather | solution.py:12
  203.0 5.2 all-gather.9
  208.2 0.2 while.100
  208.4 4.0 add_reduce_fusion.5
  212.4 4.3 exponential_reduce_fusion.2
  216.7 24.4 %all-gather.10 = f32[16384]{0:T(1024)S(1)} all-gather(f32[2048]{0:T(1024)S(1)} %add_reduce_fusion.5), channel_id=12, replica_groups=mesh['cell'=8,'desc'=4] {'cell'}, dimensions={0}, use_global_device_ids=true | all-gather | bytes 73728 | tf_op jit(solution)/shard_map/all_gather | solution.py:12
  241.2 24.3 %all-gather.11 = f32[16384]{0:T(1024)S(1)} all-gather(f32[2048]{0:T(1024)S(1)} %exponential_reduce_fusion.2), channel_id=13, replica_groups=mesh['cell'=8,'desc'=4] {'cell'}, dimensions={0}, use_global_device_ids=true | all-gather | bytes 73728 | tf_op jit(solution)/shard_map/all_gather | solution.py:12
  265.5 0.4 while.101
  265.9 4.0 add_reduce_fusion
  269.9 4.4 exponential_reduce_fusion.1
  274.3 17.6 %all-gather.12 = f32[4096]{0:T(1024)S(1)} all-gather(f32[1024]{0:T(1024)S(1)} %add_reduce_fusion), channel_id=14, replica_groups=mesh['cell'=8,'desc'=4] {'desc'}, dimensions={0}, use_global_device_ids=true | all-gather | bytes 20480 | tf_op jit(solution)/shard_map/all_gather | solution.py:12
  291.9 5.4 all-gather.13
  297.5 4.0 add_reduce_fusion.4
  301.5 4.3 exponential_reduce_fusion
  305.8 24.2 %all-gather.14 = f32[16384]{0:T(1024)S(1)} all-gather(f32[2048]{0:T(1024)S(1)} %add_reduce_fusion.4), channel_id=16, replica_groups=mesh['cell'=8,'desc'=4] {'cell'}, dimensions={0}, use_global_device_ids=true | all-gather | bytes 73728 | tf_op jit(solution)/shard_map/all_gather | solution.py:12
  330.0 24.4 %all-gather.15 = f32[16384]{0:T(1024)S(1)} all-gather(f32[2048]{0:T(1024)S(1)} %exponential_reduce_fusion), channel_id=17, replica_groups=mesh['cell'=8,'desc'=4] {'cell'}, dimensions={0}, use_global_device_ids=true | all-gather | bytes 73728 | tf_op jit(solution)/shard_map/all_gather | solution.py:12
  354.5 0.4 while.103
  354.9 4.5 multiply_reduce_fusion.3
  359.5 17.7 %psum.63 = f32[1024]{0:T(1024)S(1)} all-reduce(f32[1024]{0:T(1024)S(1)} %multiply_reduce_fusion.3), channel_id=1, replica_groups=mesh['cell'=8,'desc'=4] {'desc'}, use_global_device_ids=true, to_apply=%region_33.34 | all-reduce | flops 1024 | bytes 8192 | tf_op jit(solution)/shard_map/psum | solution.py:80
  377.1 4.7 fusion
  381.8 13.6 %psum.64 = f32[2048]{0:T(1024)S(1)} all-reduce(f32[2048]{0:T(1024)S(1)} %fusion), channel_id=1, replica_groups=mesh['cell'=8,'desc'=4] {'cell'}, use_global_device_ids=true, to_apply=%region_35.36 | all-reduce | flops 2048 | bytes 16384 | tf_op jit(solution)/shard_map/psum | solution.py:81
  395.5 4.5 multiply_reduce_fusion.2
  400.0 9.3 %psum.65 = f32[1024]{0:T(1024)S(1)} all-reduce(f32[1024]{0:T(1024)S(1)} %multiply_reduce_fusion.2), channel_id=1, replica_groups=mesh['cell'=8,'desc'=4] {'desc'}, use_global_device_ids=true, to_apply=%region_37.38 | all-reduce | flops 1024 | bytes 8192 | tf_op jit(solution)/shard_map/psum | solution.py:80
  409.3 4.6 fusion.1
  413.9 16.1 %psum.66 = f32[2048]{0:T(1024)S(1)} all-reduce(f32[2048]{0:T(1024)S(1)} %fusion.1), channel_id=1, replica_groups=mesh['cell'=8,'desc'=4] {'cell'}, use_global_device_ids=true, to_apply=%region_39.40 | all-reduce | flops 2048 | bytes 16384 | tf_op jit(solution)/shard_map/psum | solution.py:81
  430.0 4.5 multiply_reduce_fusion.1
  434.6 9.3 %psum.67 = f32[1024]{0:T(1024)S(1)} all-reduce(f32[1024]{0:T(1024)S(1)} %multiply_reduce_fusion.1), channel_id=1, replica_groups=mesh['cell'=8,'desc'=4] {'desc'}, use_global_device_ids=true, to_apply=%region_41.42 | all-reduce | flops 1024 | bytes 8192 | tf_op jit(solution)/shard_map/psum | solution.py:80
  443.9 4.6 fusion.2
  448.5 13.7 %psum.68 = f32[2048]{0:T(1024)S(1)} all-reduce(f32[2048]{0:T(1024)S(1)} %fusion.2), channel_id=1, replica_groups=mesh['cell'=8,'desc'=4] {'cell'}, use_global_device_ids=true, to_apply=%region_43.44 | all-reduce | flops 2048 | bytes 16384 | tf_op jit(solution)/shard_map/psum | solution.py:81
  462.2 4.5 multiply_reduce_fusion
  466.7 9.7 %psum.69 = f32[1024]{0:T(1024)S(1)} all-reduce(f32[1024]{0:T(1024)S(1)} %multiply_reduce_fusion), channel_id=1, replica_groups=mesh['cell'=8,'desc'=4] {'desc'}, use_global_device_ids=true, to_apply=%region_45.46 | all-reduce | flops 1024 | bytes 8192 | tf_op jit(solution)/shard_map/psum | solution.py:80
  476.4 24.1 %add_subtract_fusion = f32[1024,2048]{1,0:T(8,128)S(1)} fusion(f32[1024,2048]{1,0:T(8,128)} %copy-done.1, f32[1024]{0:T(1024)S(1)} %neg.59, f32[2048]{0:T(1024)S(1)} %get-tuple-element.338, f32[2048]{0:T(1024)S(1)} %neg.58, f32[1024]{0:T(1024)S(1)} %neg.57, f32[2048]{0:T(1024)S(1)} %get-tuple-element.340, f32[2048]{0:T(1024)S(1)} %neg.56, f32[1024]{0:T(1024)S(1)} %neg.55, ...), kind=kLoop, calls=%fused_computation.24 | loop fusion | flops 58720256 | bytes 16908288 | tf_op jit(solution)/shard_map/sub | solution.py:64
  500.5 3.2 copy-done.3
  503.7 7.6 %convolution_multiply_fusion.2 = f32[1024,256]{1,0:T(8,128)} fusion(f32[1024,2048]{1,0:T(8,128)S(1)} %add_subtract_fusion, f32[2048,256]{1,0:T(8,128)S(1)} %copy-done), kind=kOutput, calls=%fused_computation.57 | convolution fusion | flops 6442713088 | bytes 11534336 | tf_op jit(solution)/shard_map/dot_general | solution.py:83
  511.4 0.3 all-reduce.5.cloned.1.call-start
  511.7 16.5 %convolution_multiply_fusion.1 = f32[2048,256]{1,0:T(8,128)} fusion(f32[1024,2048]{1,0:T(8,128)} %copy-done.3, f32[1024,256]{1,0:T(8,128)S(1)} %copy-done.4), kind=kOutput, calls=%fused_computation.56 | convolution fusion | flops 6442975232 | bytes 11534336 | tf_op jit(solution)/shard_map/dot_general | solution.py:84
  528.2 20.7 %all-reduce.3.cloned.1.call-done = f32[1024,256]{1,0:T(8,128)} async-done(((f32[1024,256]{1,0:T(8,128)}), f32[1024,256]{1,0:T(8,128)}) %all-reduce.3.cloned.1.call-update) | async-done | bytes 1048592 | tf_op jit(solution)/shard_map/psum | solution.py:87
  549.0 105.9 %all-reduce.5.cloned.1.call-done = f32[2048,256]{1,0:T(8,128)} async-done(((f32[2048,256]{1,0:T(8,128)}), f32[2048,256]{1,0:T(8,128)}) %all-reduce.5.cloned.1.call-update) | async-done | bytes 2097168 | tf_op jit(solution)/shard_map/psum | solution.py:88
  654.9 2.3 copy.83
  657.1 3.0 copy.84
  (160 shorter events, 1.8 us)
Async XLA Ops:
  7.2 1.6 copy-start
  7.2 16.4 %copy-start.5 = (f32[2048]{0:T(1024)S(1)}, f32[2048]{0:T(1024)}, u32[]{:S(2)}) copy-start(f32[2048]{0:T(1024)} %param.23) | copy-start | bytes 24580
  7.2 541.8 %all-reduce.3.cloned.1.call-start = ((), (), s32[]{:S(2)}) async-start(), calls=%async_computation | async-start | bytes 2097152 | tf_op jit(solution)/shard_map/psum | solution.py:87
  17.8 5.7 copy-start.1
  30.9 5.8 copy-start.2
  297.5 57.5 %copy-start.6 = (f32[2048]{0:T(1024)S(1)}, f32[2048]{0:T(1024)}, u32[]{:S(2)}) copy-start(f32[2048]{0:T(1024)} %param.25) | copy-start | bytes 24580
  301.5 75.6 %copy-start.7 = (f32[1024]{0:T(1024)S(1)}, f32[1024]{0:T(1024)}, u32[]{:S(2)}) copy-start(f32[1024]{0:T(1024)} %param.24) | copy-start | bytes 12292
  500.5 3.2 copy-start.3
  503.7 8.0 %copy-start.4 = (f32[1024,256]{1,0:T(8,128)S(1)}, f32[1024,256]{1,0:T(8,128)}, u32[]{:S(2)}) copy-start(f32[1024,256]{1,0:T(8,128)} %param.21) | copy-start | bytes 3145732
  511.4 143.5 %all-reduce.5.cloned.1.call-start = ((), (), s32[]{:S(2)}) async-start(), calls=%async_computation.1 | async-start | bytes 4194304 | tf_op jit(solution)/shard_map/psum | solution.py:88
Sparse Core Ops, SparseCore 0:
  511.5 37.4 all-reduce.2
  553.2 101.6 all-reduce.4
where the time goes:
time: 679 us; the launch traced here: 667 us
  blocking collectives  364 us (54%)
  waiting for transfers between devices  127 us (19%)
  other arithmetic  115 us (17%)
  matrix products  33.2 us (5%)
  between operations  15 us (2%)
  local copies, waits for them, and re-layouts  12.6 us (2%)
    all_gather x16, blocking collectives, combined_all(): pieces = jax.tree.map(lambda part: lax.all_gather(part, axis), value)  275 us
    psum x1, waiting for transfers between devices, on_device(): grad_descs = lax.psum(part_y, 'cell')  106 us
    psum x4, blocking collectives, on_device(): lax.psum(part, 'desc')  45.9 us
    psum x3, blocking collectives, on_device(): lax.psum(part, 'cell')  43.4 us
    sub x1, other arithmetic, plan_adjoint(): lbar = lbar - (bplan * gbar[None, :] + aplan * fbar[:, None])  24.1 us
    psum x1, waiting for transfers between devices, on_device(): grad_cells = lax.psum(part_x, 'desc')  20.7 us
    reduce_sum x4, other arithmetic, plan_adjoint(): fbar = -sum_rows(jnp.sum(bplan * gbar[None, :], axis=1))  18.1 us
    dot_general x1, matrix products, on_device(): lax.dot_general(lbar, cells, (((0,), (0,)), ((), ())), precision=highest,...  16.5 us
  transfers between devices with their start and end apart: 2, of which 2 were waited for; matrix products, arithmetic and copies ran while one was open for 2% of the time, Pallas kernels for 0%

commit v1 on v0

v1 whole, which is shorter than its diff:
```python
import functools
import math

import jax
import jax.numpy as jnp
from jax import lax
from jax.experimental import pallas as pl
from jax.experimental.pallas import tpu as pltpu
from jax.sharding import PartitionSpec as P

ITERS = 4
MESH = pl.DeviceIdType.MESH
LANES = 128
F32 = jnp.float32
BF16 = jnp.bfloat16


def tree(op, parts):
    parts = list(parts)
    while len(parts) > 1:
        parts = [op(parts[i], parts[i + 1]) if i + 1 < len(parts) else parts[i] for i in range(0, len(parts), 2)]
    return parts[0]


def rotate(start, offset, count):
    return lax.rem(start + offset + count, count)


def send_all(axis, count, me, buf, send_sem, recv_sem, index):
    for off in range(1, count):
        peer = rotate(me, off, count)
        pltpu.make_async_remote_copy(
            src_ref=buf.at[index, me],
            dst_ref=buf.at[index, me],
            send_sem=send_sem.at[index, off],
            recv_sem=recv_sem.at[index, me],
            device_id={axis: peer},
            device_id_type=MESH,
        ).start()


def wait_all(axis, count, me, buf, send_sem, recv_sem, index):
    for off in range(1, count):
        source = rotate(me, -off, count)
        peer = rotate(me, off, count)
        got = pltpu.make_async_remote_copy(
            src_ref=buf.at[index, source],
            dst_ref=buf.at[index, source],
            send_sem=send_sem.at[index, off],
            recv_sem=recv_sem.at[index, source],
            device_id={axis: peer},
            device_id_type=MESH,
        )
        got.wait_recv()
        got.wait_send()


def split(value):
    high = value.astype(BF16)
    return high, (value - high.astype(F32)).astype(BF16)


def dot3(a_high, a_low, b_high, b_low):
    dot = functools.partial(jnp.dot, preferred_element_type=F32)
    return dot(a_high, b_high) + (dot(a_low, b_high) + dot(a_high, b_low))


def plan_kernel(
    n_cell, n_desc,
    cells, descs, g_first, cf, cg,
    px, py,
    logit, bplan, lbar, vcol, racc_m, racc_s, cacc_m, cacc_s, wide_a, wide_b,
    f_all, g_all, gbar, d_high, d_low, c_high, c_low,
    row_buf, col_buf, fbar_buf, gbar_buf,
    row_send, row_recv, col_send, col_recv, fb_send, fb_recv, gb_send, gb_recv,
):
    rows, width = cells.shape
    cols = descs.shape[0]
    scale = 2.0 / math.sqrt(width)
    my_cell = lax.axis_index("cell")
    my_desc = lax.axis_index("desc")
    blocks = cols // LANES
    group = 16
    unroll = 4

    barrier = pltpu.get_barrier_semaphore()
    for off in range(1, n_desc):
        pl.semaphore_signal(barrier, inc=1, device_id={"desc": rotate(my_desc, off, n_desc)}, device_id_type=MESH)
    for off in range(1, n_cell):
        pl.semaphore_signal(barrier, inc=1, device_id={"cell": rotate(my_cell, off, n_cell)}, device_id_type=MESH)

    def multiply(i, _):
        at = pl.ds(pl.multiple_of(i * 256, 256), 256)
        logit[at, :] = scale * lax.dot_general(
            cells[at, :], descs[...], (((1,), (1,)), ((), ())),
            precision=lax.Precision.HIGHEST, preferred_element_type=F32,
        )
        return 0

    lax.fori_loop(0, rows // 256, multiply, 0)
    g_all[0] = g_first[...]
    gbar[...] = cg[...]
    pl.semaphore_wait(barrier, n_desc + n_cell - 2)

    def spread_rows(vector):
        vcol[...] = jnp.broadcast_to(vector, (LANES, rows)).T

    def lane(b):
        return slice(b * LANES, (b + 1) * LANES)

    def forward(k, _):
        wide_a[...] = jnp.broadcast_to(g_all[k], (8, cols))

        def row_pass(i, _):
            for u in range(unroll):
                at = pl.ds(pl.multiple_of((i * unroll + u) * 8, 8), 8)
                parts = [logit[at, lane(b)] + wide_a[:, lane(b)] for b in range(blocks)]
                top = tree(jnp.maximum, parts)
                racc_m[at, :] = top
                racc_s[at, :] = tree(jnp.add, [jnp.exp(part - top) for part in parts])
            return 0

        lax.fori_loop(0, rows // (8 * unroll), row_pass, 0)
        tops = racc_m[...].T
        top = jnp.max(tops, axis=0, keepdims=True)
        row_buf[k, my_desc, 0:1, :] = top
        row_buf[k, my_desc, 1:2, :] = jnp.sum(racc_s[...].T * jnp.exp(tops - top), axis=0, keepdims=True)
        send_all("desc", n_desc, my_desc, row_buf, row_send, row_recv, k)
        wait_all("desc", n_desc, my_desc, row_buf, row_send, row_recv, k)
        tops = [row_buf[k, p, 0:1, :] for p in range(n_desc)]
        top = tree(jnp.maximum, tops)
        total = tree(jnp.add, [row_buf[k, p, 1:2, :] * jnp.exp(tops[p] - top) for p in range(n_desc)])
        f_now = -(top + jnp.log(total))
        f_all[k] = f_now
        spread_rows(f_now)
        cacc_m[...] = jnp.full((8, cols), -jnp.inf, F32)
        cacc_s[...] = jnp.zeros((8, cols), F32)

        def col_pass(i, _):
            base = i * (8 * group)
            for b in range(blocks):
                ats = [pl.ds(pl.multiple_of(base + 8 * u, 8), 8) for u in range(group)]
                parts = [logit[at, lane(b)] + vcol[at, :] for at in ats]
                before = cacc_m[:, lane(b)]
                top = jnp.maximum(before, tree(jnp.maximum, parts))
                cacc_m[:, lane(b)] = top
                cacc_s[:, lane(b)] = cacc_s[:, lane(b)] * jnp.exp(before - top) + tree(
                    jnp.add, [jnp.exp(part - top) for part in parts]
                )
            return 0

        lax.fori_loop(0, rows // (8 * group), col_pass, 0)
        top = jnp.max(cacc_m[...], axis=0, keepdims=True)
        col_buf[k, my_cell, 0:1, :] = top
        col_buf[k, my_cell, 1:2, :] = jnp.sum(cacc_s[...] * jnp.exp(cacc_m[...] - top), axis=0, keepdims=True)
        send_all("cell", n_cell, my_cell, col_buf, col_send, col_recv, k)
        wait_all("cell", n_cell, my_cell, col_buf, col_send, col_recv, k)
        tops = [col_buf[k, p, 0:1, :] for p in range(n_cell)]
        top = tree(jnp.maximum, tops)
        total = tree(jnp.add, [col_buf[k, p, 1:2, :] * jnp.exp(tops[p] - top) for p in range(n_cell)])
        g_all[k + 1] = -(top + jnp.log(total))
        return 0

    lax.fori_loop(0, ITERS, forward, 0)

    def backward(t, _):
        k = ITERS - 1 - t
        wide_a[...] = jnp.broadcast_to(g_all[k + 1], (8, cols))
        wide_b[...] = jnp.broadcast_to(gbar[...], (8, cols))
        spread_rows(f_all[k])

        def row_pass(i, _):
            for u in range(unroll):
                at = pl.ds(pl.multiple_of((i * unroll + u) * 8, 8), 8)
                f_here = vcol[at, :]
                terms = []
                for b in range(blocks):
                    value = jnp.exp((logit[at, lane(b)] + f_here) + wide_a[:, lane(b)])
                    bplan[at, lane(b)] = value
                    terms.append(value * wide_b[:, lane(b)])
                racc_s[at, :] = tree(jnp.add, terms)
            return 0

        lax.fori_loop(0, rows // (8 * unroll), row_pass, 0)
        fbar_buf[k, my_desc] = jnp.sum(racc_s[...].T, axis=0, keepdims=True)
        send_all("desc", n_desc, my_desc, fbar_buf, fb_send, fb_recv, k)
        wait_all("desc", n_desc, my_desc, fbar_buf, fb_send, fb_recv, k)
        fbar = -tree(jnp.add, [fbar_buf[k, p] for p in range(n_desc)])
        fbar = fbar + jnp.where(t == 0, cf[...], 0.0)
        spread_rows(fbar)
        ratio = jnp.exp(g_all[k] - g_all[k + 1])
        wide_a[...] = jnp.broadcast_to(ratio, (8, cols))
        cacc_s[...] = jnp.zeros((8, cols), F32)

        def col_pass(first):
            def body(i, _):
                base = i * (8 * group)
                for b in range(blocks):
                    terms = []
                    for u in range(group):
                        at = pl.ds(pl.multiple_of(base + 8 * u, 8), 8)
                        value = bplan[at, lane(b)]
                        term = value * vcol[at, :]
                        terms.append(term)
                        update = value * wide_b[:, lane(b)] + term * wide_a[:, lane(b)]
                        lbar[at, lane(b)] = -update if first else lbar[at, lane(b)] - update
                    cacc_s[:, lane(b)] = cacc_s[:, lane(b)] + tree(jnp.add, terms)
                return 0

            lax.fori_loop(0, rows // (8 * group), body, 0)

        @pl.when(t == 0)
        def _():
            col_pass(True)

        @pl.when(t > 0)
        def _():
            col_pass(False)

        @pl.when(t < ITERS - 1)
        def _():
            gbar_buf[k, my_cell] = jnp.sum(cacc_s[...], axis=0, keepdims=True)
            send_all("cell", n_cell, my_cell, gbar_buf, gb_send, gb_recv, k)
            wait_all("cell", n_cell, my_cell, gbar_buf, gb_send, gb_recv, k)
            total = tree(jnp.add, [gbar_buf[k, p] for p in range(n_cell)])
            gbar[...] = -(jnp.exp(g_all[k] - g_all[k + 1]) * total)

        return 0

    lax.fori_loop(0, ITERS, backward, 0)

    d_high[...], d_low[...] = split(descs[...])
    c_high[...], c_low[...] = split(cells[...].T)

    def cells_side(i, _):
        at = pl.ds(pl.multiple_of(i * 256, 256), 256)
        high, low = split(lbar[at, :])
        px[at, :] = scale * dot3(high, low, d_high[...], d_low[...])
        return 0

    lax.fori_loop(0, rows // 256, cells_side, 0)

    def descs_side(i, _):
        at = pl.ds(pl.multiple_of(i * 256, 256), 256)
        high, low = split(lbar[:, at])
        py[at, :] = (scale * dot3(c_high[...], c_low[...], high, low)).T
        return 0

    lax.fori_loop(0, cols // 256, descs_side, 0)


def run_plan(n_cell, n_desc, cells, descs, g_start, cot_f, cot_g):
    rows, width = cells.shape
    cols = descs.shape[0]
    vmem = pltpu.VMEM
    dma = pltpu.SemaphoreType.DMA
    spec = pl.BlockSpec(memory_space=pltpu.VMEM)
    return pl.pallas_call(
        functools.partial(plan_kernel, n_cell, n_desc),
        out_shape=(
            jax.ShapeDtypeStruct((rows, width), F32),
            jax.ShapeDtypeStruct((cols, width), F32),
        ),
        in_specs=[spec] * 5,
        out_specs=(spec, spec),
        scratch_shapes=[
            vmem((rows, cols), F32),
            vmem((rows, cols), F32),
            vmem((rows, cols), F32),
            vmem((rows, LANES), F32),
            vmem((rows, LANES), F32),
            vmem((rows, LANES), F32),
            vmem((8, cols), F32),
            vmem((8, cols), F32),
            vmem((8, cols), F32),
            vmem((8, cols), F32),
            vmem((ITERS, 1, rows), F32),
            vmem((ITERS + 1, 1, cols), F32),
            vmem((1, cols), F32),
            vmem((cols, width), BF16),
            vmem((cols, width), BF16),
            vmem((width, rows), BF16),
            vmem((width, rows), BF16),
            vmem((ITERS, n_desc, 2, rows), F32),
            vmem((ITERS, n_cell, 2, cols), F32),
            vmem((ITERS, n_desc, 1, rows), F32),
            vmem((ITERS, n_cell, 1, cols), F32),
            dma((ITERS, n_desc)),
            dma((ITERS, n_desc)),
            dma((ITERS, n_cell)),
            dma((ITERS, n_cell)),
            dma((ITERS, n_desc)),
            dma((ITERS, n_desc)),
            dma((ITERS, n_cell)),
            dma((ITERS, n_cell)),
        ],
        compiler_params=pltpu.CompilerParams(
            collective_id=0, has_side_effects=True, vmem_limit_bytes=60 * 1024 * 1024
        ),
        name="plan",
    )(cells, descs, g_start[None, :], cot_f[None, :], cot_g[None, :])


def solution(mesh):
    n_cell = mesh.shape["cell"]
    n_desc = mesh.shape["desc"]

    def on_device(cells, descs, g_start, cot_f, cot_g):
        part_x, part_y = run_plan(n_cell, n_desc, cells, descs, g_start, cot_f, cot_g)
        return (lax.psum(part_x, "desc"), lax.psum(part_y, "cell"))

    placed = (P("cell", None), P("desc", None), P("desc"), P("cell"), P("desc"))
    return jax.shard_map(
        on_device,
        mesh=mesh,
        in_specs=placed,
        out_specs=(P("cell", None), P("desc", None)),
        check_vma=False,
    )
```

time: 679 us -> 289 us (0.43); the launches traced: 667 us -> 285 us
  blocking collectives: 364 us -> 0 us
  Pallas kernels: 0 us -> 126 us
  other arithmetic: 115 us -> 0 us
  matrix products: 33.2 us -> 0 us
  waiting for transfers between devices: 127 us -> 142 us
  local copies, waits for them, and re-layouts: 12.6 us -> 3.73 us
    all_gather x16 -> x0, blocking collectives: 275 us -> none  [combined_all(): pieces = jax.tree.map(lambda part: lax.all_gather(part, axis), value)]
    pallas_call x0 -> x1, Pallas kernels: none -> 126 us  [run_plan(): pl.pallas_call(functools.partial(plan_kernel, n_cell, n_desc), out_shape=...]
    psum x7 -> x0, blocking collectives: 89.4 us -> none  [the longest x4 45.9 us: on_device(): lax.psum(part, 'desc')]
    reduce_sum x15 -> x0, other arithmetic: 61.8 us -> none  [the longest x4 18.1 us: plan_adjoint(): fbar = -sum_rows(jnp.sum(bplan * gbar[None, :], axis=1))]
    dot_general x3 -> x0, matrix products: 33.2 us -> none  [the longest x1 16.5 us: on_device(): lax.dot_general(lbar, cells, (((0,), (0,)), ((), ())), precision=highest,...]
    reduce_max x7 -> x0, other arithmetic: 28.2 us -> none  [the longest x4 16.2 us: plan_adjoint(): col_max = jnp.max(wvals, axis=0)]
    sub x1 -> x0, other arithmetic: 24.1 us -> none  [plan_adjoint(): lbar = lbar - (bplan * gbar[None, :] + aplan * fbar[:, None])]
    psum x2, waiting for transfers between devices: 127 us -> 141 us  [on_device(): return (lax.psum(part_x, 'desc'), lax.psum(part_y, 'cell'))]
  transfers between devices with their start and end apart: 2 -> 2, of which waited for: 2 -> 2; matrix products, arithmetic and copies ran while one was open for 2% -> 0% of each run, Pallas kernels for 0% -> 0%
where the time goes in v1:
time: 289 us; the launch traced here: 285 us
  waiting for transfers between devices  142 us (49%)
  Pallas kernels  126 us (44%)
  between operations  14 us (5%)
  local copies, waits for them, and re-layouts  3.73 us (1%)
    psum x2, waiting for transfers between devices, on_device(): return (lax.psum(part_x, 'desc'), lax.psum(part_y, 'cell'))  141 us
    pallas_call x1, Pallas kernels, run_plan(): pl.pallas_call(functools.partial(plan_kernel, n_cell, n_desc), out_shape=...  126 us
  transfers between devices with their start and end apart: 2, of which 2 were waited for; matrix products, arithmetic and copies ran while one was open for 0% of the time, Pallas kernels for 0%

profile of v1, /device:TPU:27, one launch (start us, length us, event | category | flops | bytes accessed | tf_op | source)
XLA Modules:
  0.0 285.4 jit_solution(10619296497857196255)
XLA Ops:
  7.2 0.0 all-reduce.3.cloned.1.call-start
  7.2 125.7 %plan.1 = (f32[1024,256]{1,0:T(8,128)}, f32[2048,256]{1,0:T(8,128)}) custom-call(f32[1024,256]{1,0:T(8,128)} %cells.1, f32[2048,256]{1,0:T(8,128)} %descs.1, f32[1,2048]{1,0:T(1,128)} %bitcast.3, f32[1,1024]{1,0:T(1,128)} %bitcast.5, f32[1,2048]{1,0:T(1,128)} %bitcast.4), custom_call_target="tpu_custom_call" | custom-call | tf_op jit(solution)/shard_map/plan/pallas_call | solution.py:258
  132.9 0.0 all-reduce.3.cloned.1.call-update
  132.9 0.0 all-reduce.5.cloned.1.call-start
  133.0 0.7 all-reduce.5.cloned.1.call-update
  133.7 35.8 %all-reduce.3.cloned.1.call-done = f32[1024,256]{1,0:T(8,128)} async-done(((f32[1024,256]{1,0:T(8,128)}), f32[1024,256]{1,0:T(8,128)}) %all-reduce.3.cloned.1.call-update) | async-done | bytes 1048592 | tf_op jit(solution)/shard_map/psum | solution.py:310
  169.5 105.3 %all-reduce.5.cloned.1.call-done = f32[2048,256]{1,0:T(8,128)} async-done(((f32[2048,256]{1,0:T(8,128)}), f32[2048,256]{1,0:T(8,128)}) %all-reduce.5.cloned.1.call-update) | async-done | bytes 2097168 | tf_op jit(solution)/shard_map/psum | solution.py:310
  274.8 0.0 copy-start
  274.8 2.4 copy.11
  277.2 0.0 copy-done
  277.2 1.3 copy.12
Async XLA Ops:
  7.2 162.3 %all-reduce.3.cloned.1.call-start = ((), (), s32[]{:S(2)}) async-start(), calls=%async_computation | async-start | bytes 2097152 | tf_op jit(solution)/shard_map/psum | solution.py:310
  132.9 141.9 %all-reduce.5.cloned.1.call-start = ((), (), s32[]{:S(2)}) async-start(), calls=%async_computation.1 | async-start | bytes 4194304 | tf_op jit(solution)/shard_map/psum | solution.py:310
  274.8 2.4 copy-start
Sparse Core Ops, SparseCore 0:
  133.0 36.3 all-reduce.2
  173.1 101.6 all-reduce.4

commit v2 on v1

--- a/solution.py
+++ b/solution.py
@@ -73,6 +73,7 @@
     f_all, g_all, gbar, d_high, d_low, c_high, c_low,
     row_buf, col_buf, fbar_buf, gbar_buf,
     row_send, row_recv, col_send, col_recv, fb_send, fb_recv, gb_send, gb_recv,
+    part_x, got_x, part_y, got_y, x_send, x_recv, y_send, y_recv,
 ):
     rows, width = cells.shape
     cols = descs.shape[0]
@@ -80,6 +81,8 @@
     my_cell = lax.axis_index("cell")
     my_desc = lax.axis_index("desc")
     blocks = cols // LANES
+    x_block = rows // n_desc
+    y_block = cols // n_cell
     group = 16
     unroll = 4
 
@@ -232,21 +235,82 @@
     d_high[...], d_low[...] = split(descs[...])
     c_high[...], c_low[...] = split(cells[...].T)
 
-    def cells_side(i, _):
-        at = pl.ds(pl.multiple_of(i * 256, 256), 256)
+    my_rows = pl.ds(pl.multiple_of(my_desc * x_block, x_block), x_block)
+    my_cols = pl.ds(pl.multiple_of(my_cell * y_block, y_block), y_block)
+
+    def y_tile(owner):
+        at = pl.ds(pl.multiple_of(owner * y_block, y_block), y_block)
+        high, low = split(lbar[:, at])
+        return (scale * dot3(c_high[...], c_low[...], high, low)).T
+
+    def x_tile(owner):
+        at = pl.ds(pl.multiple_of(owner * x_block, x_block), x_block)
         high, low = split(lbar[at, :])
-        px[at, :] = scale * dot3(high, low, d_high[...], d_low[...])
-        return 0
-
-    lax.fori_loop(0, rows // 256, cells_side, 0)
-
-    def descs_side(i, _):
-        at = pl.ds(pl.multiple_of(i * 256, 256), 256)
-        high, low = split(lbar[:, at])
-        py[at, :] = (scale * dot3(c_high[...], c_low[...], high, low)).T
-        return 0
-
-    lax.fori_loop(0, cols // 256, descs_side, 0)
+        return scale * dot3(high, low, d_high[...], d_low[...])
+
+    def scatter_copy(axis, part, got, send_sem, recv_sem, peer, slot, off):
+        return pltpu.make_async_remote_copy(
+            src_ref=part.at[peer],
+            dst_ref=got.at[slot],
+            send_sem=send_sem.at[0, off],
+            recv_sem=recv_sem.at[0, slot],
+            device_id={axis: peer},
+            device_id_type=MESH,
+        )
+
+    def gather_copy(axis, out, send_sem, recv_sem, peer, slot, off, size):
+        at = pl.ds(pl.multiple_of(slot * size, size), size)
+        return pltpu.make_async_remote_copy(
+            src_ref=out.at[at],
+            dst_ref=out.at[at],
+            send_sem=send_sem.at[1, off],
+            recv_sem=recv_sem.at[1, slot],
+            device_id={axis: peer},
+            device_id_type=MESH,
+        )
+
+    def send_y(off, _):
+        owner = rotate(my_cell, off, n_cell)
+        part_y[owner] = y_tile(owner)
+        scatter_copy("cell", part_y, got_y, y_send, y_recv, owner, my_cell, off).start()
+        return 0
+
+    def send_x(off, _):
+        owner = rotate(my_desc, off, n_desc)
+        part_x[owner] = x_tile(owner)
+        scatter_copy("desc", part_x, got_x, x_send, x_recv, owner, my_desc, off).start()
+        return 0
+
+    lax.fori_loop(1, n_cell, send_y, 0)
+    lax.fori_loop(1, n_desc, send_x, 0)
+    got_y[my_cell] = y_tile(my_cell)
+    got_x[my_desc] = x_tile(my_desc)
+
+    def finish_scatter(axis, count, me, part, got, send_sem, recv_sem):
+        for off in range(1, count):
+            peer = rotate(me, off, count)
+            scatter_copy(axis, part, got, send_sem, recv_sem, peer, rotate(me, -off, count), off).wait_recv()
+
+    def start_gather(axis, count, me, out, send_sem, recv_sem, size):
+        for off in range(1, count):
+            gather_copy(axis, out, send_sem, recv_sem, rotate(me, off, count), me, off, size).start()
+
+    finish_scatter("desc", n_desc, my_desc, part_x, got_x, x_send, x_recv)
+    px[my_rows, :] = tree(jnp.add, [got_x[p] for p in range(n_desc)])
+    start_gather("desc", n_desc, my_desc, px, x_send, x_recv, x_block)
+    finish_scatter("cell", n_cell, my_cell, part_y, got_y, y_send, y_recv)
+    py[my_cols, :] = tree(jnp.add, [got_y[p] for p in range(n_cell)])
+    start_gather("cell", n_cell, my_cell, py, y_send, y_recv, y_block)
+    for axis, count, me, part, got, out, send_sem, recv_sem, size in (
+        ("desc", n_desc, my_desc, part_x, got_x, px, x_send, x_recv, x_block),
+        ("cell", n_cell, my_cell, part_y, got_y, py, y_send, y_recv, y_block),
+    ):
+        for off in range(1, count):
+            peer = rotate(me, off, count)
+            source = rotate(me, -off, count)
+            gather_copy(axis, out, send_sem, recv_sem, peer, source, off, size).wait_recv()
+            scatter_copy(axis, part, got, send_sem, recv_sem, peer, source, off).wait_send()
+            gather_copy(axis, out, send_sem, recv_sem, peer, me, off, size).wait_send()
 
 
 def run_plan(n_cell, n_desc, cells, descs, g_start, cot_f, cot_g):
@@ -293,6 +357,14 @@
             dma((ITERS, n_desc)),
             dma((ITERS, n_cell)),
             dma((ITERS, n_cell)),
+            vmem((n_desc, rows // n_desc, width), F32),
+            vmem((n_desc, rows // n_desc, width), F32),
+            vmem((n_cell, cols // n_cell, width), F32),
+            vmem((n_cell, cols // n_cell, width), F32),
+            dma((2, n_desc)),
+            dma((2, n_desc)),
+            dma((2, n_cell)),
+            dma((2, n_cell)),
         ],
         compiler_params=pltpu.CompilerParams(
             collective_id=0, has_side_effects=True, vmem_limit_bytes=60 * 1024 * 1024
@@ -306,8 +378,7 @@
     n_desc = mesh.shape["desc"]
 
     def on_device(cells, descs, g_start, cot_f, cot_g):
-        part_x, part_y = run_plan(n_cell, n_desc, cells, descs, g_start, cot_f, cot_g)
-        return (lax.psum(part_x, "desc"), lax.psum(part_y, "cell"))
+        return run_plan(n_cell, n_desc, cells, descs, g_start, cot_f, cot_g)
 
     placed = (P("cell", None), P("desc", None), P("desc"), P("cell"), P("desc"))
     return jax.shard_map(

time: 289 us -> 224 us (0.78); the launches traced: 285 us -> 223 us
  waiting for transfers between devices: 142 us -> 0 us
  Pallas kernels: 126 us -> 219 us
  between operations: 14 us -> 0.65 us
    psum x2 -> x0, waiting for transfers between devices: 141 us -> none  [on_device(): return (lax.psum(part_x, 'desc'), lax.psum(part_y, 'cell'))]
    pallas_call x1, Pallas kernels: 126 us -> 219 us  [run_plan(): pl.pallas_call(functools.partial(plan_kernel, n_cell, n_desc), out_shape=...]
  transfers between devices with their start and end apart: 2 -> 0, of which waited for: 2 -> 0; matrix products, arithmetic and copies ran while one was open for 0% -> 0% of each run, Pallas kernels for 0% -> 0%
where the time goes in v2:
time: 224 us; the launch traced here: 223 us
  Pallas kernels  219 us (98%)
  local copies, waits for them, and re-layouts  3.73 us (2%)
    pallas_call x1, Pallas kernels, run_plan(): pl.pallas_call(functools.partial(plan_kernel, n_cell, n_desc), out_shape=...  219 us

profile of v2, /device:TPU:27, one launch (start us, length us, event | category | flops | bytes accessed | tf_op | source)
XLA Modules:
  0.0 223.4 jit_solution(7090007815420700611)
XLA Ops:
  0.6 219.0 %plan.1 = (f32[1024,256]{1,0:T(8,128)}, f32[2048,256]{1,0:T(8,128)}) custom-call(f32[1024,256]{1,0:T(8,128)} %cells.1, f32[2048,256]{1,0:T(8,128)} %descs.1, f32[1,2048]{1,0:T(1,128)} %bitcast.3, f32[1,1024]{1,0:T(1,128)} %bitcast.5, f32[1,2048]{1,0:T(1,128)} %bitcast.4), custom_call_target="tpu_custom_call" | custom-call | tf_op jit(solution)/shard_map/plan/pallas_call | solution.py:322
  219.6 0.0 copy-start
  219.6 2.4 %copy.9 = f32[1024,256]{1,0:T(8,128)} copy(f32[1024,256]{1,0:T(8,128)} %get-tuple-element.4) | data formatting | bytes 2097152
  222.0 0.0 copy-done
  222.0 1.3 copy.10
Async XLA Ops:
  219.6 2.4 %copy-start = (f32[2048,256]{1,0:T(8,128)S(1)}, f32[2048,256]{1,0:T(8,128)}, u32[]{:S(2)}) copy-start(f32[2048,256]{1,0:T(8,128)} %get-tuple-element.5) | copy-start | bytes 6291460
